TPU v7x, 32 devices: a whole 2x2x4 slice. The times are simulated.
32 devices in a mesh: grp: 4 (over z), band: 8 (over y, x, core).
Axes of the slice: x: 2, y: 2, z: 4, core: 2. Of those that a mesh axis runs over, the one named last changes fastest.
Arguments:
- latent: bfloat16 [16384, 512], P(('grp', 'band')), may hold values from -6 to 6
- obs_feat: bfloat16 [4096, 512], P(('grp', 'band')), may hold values from -6 to 6
- obs_bias: bfloat16 [4096], P(('grp', 'band')), may hold values from -240 to 240
- obs_route: int32 [512, 1], P(('grp', 'band')), may hold values from 0 to 7; in each aligned block of 16 rows (0 to 15, 16 to 31, ...) at most 2 rows name the same one
- obs_tile_mask: int32 [512, 8], P(('grp', 'band')), may hold values 0 or 1
- w_query: bfloat16 [512, 512], replicated, may hold values from -0.25 to 0.25
- w_key: bfloat16 [512, 512], replicated, may hold values from -0.25 to 0.25
- w_value: bfloat16 [512, 512], replicated, may hold values from -0.25 to 0.25
- w_out: bfloat16 [512, 512], replicated, may hold values from -0.25 to 0.25
- grad_out: bfloat16 [16384, 512], P(('grp', 'band')), may hold values from -6 to 6
Outputs:
- attended: bfloat16 [16384, 512], P(('grp', 'band'))
- grad_latent: bfloat16 [16384, 512], P(('grp', 'band'))
- grad_obs: bfloat16 [4096, 512], P(('grp', 'band'))
- grad_weights: float32 [2048, 512], P('band')
Inputs may be any that keep to these rules, and one draw needn't show every extreme that they name: `obs_route`: among the 16 blocks of one device no band is named more than 2 times, a bound that some block reaches by some device in every draw.
All inputs are finite; a program needn't handle non-finite values. No bound on the sum of `obs_tile_mask` on one device may be relied on, other than what follows from the above.
Results may differ from a plain program's by a relative error of at most 0.023.
Values may be sent and summed in bfloat16 or wider, within the bound.
A program may use at most 64 MiB of HBM per device.

v0:
```python
import math

import jax
import jax.numpy as jnp
from jax import lax
from jax.sharding import PartitionSpec as P

HEADS = 16
QTILE = 64
OB = 8
SRC_BLK = 16
CAP = 2


def band_attention(query, dattn, keys, values, key_bias, visible, head_size):
    scale = 1.0 / math.sqrt(head_size)
    lat_rows = query.shape[0]
    key_rows = keys.shape[0]
    group_width = 4 * head_size

    def per_group(index):
        start = index * group_width
        query_g = lax.dynamic_slice_in_dim(query, start, group_width, 1).reshape(
            lat_rows, 4, head_size
        )
        dattn_g = lax.dynamic_slice_in_dim(dattn, start, group_width, 1).reshape(
            lat_rows, 4, head_size
        )
        keys_g = lax.dynamic_slice_in_dim(keys, start, group_width, 1).reshape(
            key_rows, 4, head_size
        )
        values_g = lax.dynamic_slice_in_dim(values, start, group_width, 1).reshape(
            key_rows, 4, head_size
        )
        scores = (
            jnp.einsum("qhd,khd->hqk", query_g, keys_g, preferred_element_type=jnp.float32) * scale
            + key_bias[None, None, :]
        )
        masked = jnp.where(visible[None], scores, -jnp.inf)
        top = jnp.maximum(jnp.max(masked, axis=-1), 0.0)
        expo = jnp.where(visible[None], jnp.exp(scores - top[..., None]), 0.0)
        total = jnp.exp(-top) + jnp.sum(expo, axis=-1)
        prob = expo / total[..., None]
        prob_b = prob.astype(jnp.bfloat16)
        attn_g = jnp.einsum("hqk,khd->qhd", prob_b, values_g, preferred_element_type=jnp.float32)
        dprob = jnp.einsum("qhd,khd->hqk", dattn_g, values_g, preferred_element_type=jnp.float32)
        delta = jnp.sum(prob * dprob, axis=-1)
        dscore = (prob * (dprob - delta[..., None])).astype(jnp.bfloat16)
        dquery_g = (
            jnp.einsum("hqk,khd->qhd", dscore, keys_g, preferred_element_type=jnp.float32) * scale
        )
        dkeys_g = (
            jnp.einsum("hqk,qhd->khd", dscore, query_g, preferred_element_type=jnp.float32) * scale
        )
        dvalues_g = jnp.einsum("hqk,qhd->khd", prob_b, dattn_g, preferred_element_type=jnp.float32)
        return (
            attn_g.reshape(lat_rows, group_width).astype(jnp.bfloat16),
            dquery_g.reshape(lat_rows, group_width).astype(jnp.bfloat16),
            dkeys_g.reshape(key_rows, group_width).astype(jnp.bfloat16),
            dvalues_g.reshape(key_rows, group_width).astype(jnp.bfloat16),
        )

    groups = query.shape[1] // group_width
    stacked = lax.map(per_group, jnp.arange(groups))

    def unstack(piece):
        return jnp.transpose(piece, (1, 0, 2)).reshape(piece.shape[1], groups * group_width)

    return tuple((unstack(piece) for piece in stacked))


def per_device(
    latent, obs_feat, obs_bias, obs_route, obs_tile_mask, w_query, w_key, w_value, w_out, grad_out
):
    band_count = lax.axis_size("band")
    group_count = lax.axis_size("grp")
    slots = band_count * CAP
    lat_rows = latent.shape[0]
    width = latent.shape[1]
    head_size = width // HEADS
    tile_count = obs_tile_mask.shape[1]
    route = obs_route[:, 0]
    order = jnp.arange(SRC_BLK)
    earlier = order[:, None] < order[None, :]
    rank = jnp.sum(((route[:, None] == route[None, :]) & earlier).astype(jnp.int32), axis=0)
    position = route * CAP + rank
    placing = (jnp.arange(slots)[:, None] == position[None, :]).astype(jnp.bfloat16)
    send_bias = jnp.dot(
        placing, obs_bias.reshape(SRC_BLK, OB), preferred_element_type=jnp.float32
    ).astype(jnp.bfloat16)
    send_mask = jnp.dot(
        placing, obs_tile_mask.astype(jnp.bfloat16), preferred_element_type=jnp.float32
    ).astype(jnp.bfloat16)
    w_pair = jnp.concatenate([w_key, w_value], axis=1)
    send_feat = jnp.dot(
        placing, obs_feat.reshape(SRC_BLK, OB * width), preferred_element_type=jnp.float32
    ).astype(jnp.bfloat16)
    recv_feat, recv_bias, recv_mask = (
        lax.all_to_all(send_feat, "band", split_axis=0, concat_axis=0, tiled=True),
        lax.all_to_all(send_bias, "band", split_axis=0, concat_axis=0, tiled=True),
        lax.all_to_all(send_mask, "band", split_axis=0, concat_axis=0, tiled=True),
    )
    recv_rows = recv_feat.reshape(slots * OB, width)
    arrived = jnp.dot(recv_rows, w_pair, preferred_element_type=jnp.float32).astype(jnp.bfloat16)
    keys = arrived[:, :width]
    values = arrived[:, width:]
    key_bias = recv_bias.reshape(slots * OB).astype(jnp.float32)
    row_tile = jnp.arange(lat_rows) // QTILE
    tile_pick = (row_tile[:, None] == jnp.arange(tile_count)[None, :]).astype(jnp.bfloat16)
    slot_seen = jnp.dot(tile_pick, recv_mask.T, preferred_element_type=jnp.float32) > 0.5
    visible = jnp.broadcast_to(slot_seen[:, :, None], (lat_rows, slots, OB)).reshape(
        lat_rows, slots * OB
    )
    query = jnp.dot(latent, w_query, preferred_element_type=jnp.float32).astype(jnp.bfloat16)
    dattn = jnp.dot(grad_out, w_out.T, preferred_element_type=jnp.float32).astype(jnp.bfloat16)
    attn, dquery, dkeys, dvalues = band_attention(
        query, dattn, keys, values, key_bias, visible, head_size
    )
    attended = jnp.dot(attn, w_out, preferred_element_type=jnp.float32).astype(jnp.bfloat16)
    grad_latent = jnp.dot(dquery, w_query.T, preferred_element_type=jnp.float32).astype(
        jnp.bfloat16
    )
    dpair_slots = jnp.concatenate([dkeys, dvalues], axis=1)
    feat_grad = jnp.dot(dpair_slots, w_pair.T, preferred_element_type=jnp.float32).astype(
        jnp.bfloat16
    )
    returned = lax.all_to_all(
        feat_grad.reshape(slots, OB * width), "band", split_axis=0, concat_axis=0, tiled=True
    )
    grad_obs = (
        jnp.dot(placing.T, returned, preferred_element_type=jnp.float32)
        .astype(jnp.bfloat16)
        .reshape(SRC_BLK * OB, width)
    )
    grad_pair = jnp.einsum("ri,rj->ij", recv_rows, dpair_slots, preferred_element_type=jnp.float32)
    grad_wq = jnp.einsum("ri,rj->ij", latent, dquery, preferred_element_type=jnp.float32)
    grad_wo = jnp.einsum("ri,rj->ij", attn, grad_out, preferred_element_type=jnp.float32)
    term = jnp.concatenate(
        [grad_wq, grad_pair[:, :width], grad_pair[:, width:], grad_wo], axis=0
    ) / float(group_count)
    band_rows = lax.psum_scatter(term.astype(jnp.bfloat16), "band", scatter_dimension=0, tiled=True)
    grads = lax.psum(band_rows, "grp").astype(jnp.float32)
    return (attended, grad_latent, grad_obs, grads)


def solution(mesh):
    return jax.shard_map(
        per_device,
        mesh=mesh,
        in_specs=(
            P(("grp", "band"), None),
            P(("grp", "band"), None),
            P(("grp", "band")),
            P(("grp", "band"), None),
            P(("grp", "band"), None),
            P(),
            P(),
            P(),
            P(),
            P(("grp", "band"), None),
        ),
        out_specs=(
            P(("grp", "band"), None),
            P(("grp", "band"), None),
            P(("grp", "band"), None),
            P("band", None),
        ),
        check_vma=False,
    )
```

profile of v0, /device:TPU:0, one launch (start us, length us, event | category | flops | bytes accessed | tf_op | source)
XLA Modules:
  0.0 164.6 jit_solution(14191782597755601926)
XLA Ops:
  7.2 0.9 convert_reduce_fusion
  8.7 0.7 reshape.147
  10.3 5.2 %all-to-all-start.2 = ((bf16[8,2,8]{2,1,0:T(2,128)(2,1)}), bf16[8,2,8]{2,1,0:T(2,128)(2,1)S(1)}, u32[]{:S(2)}, u32[]{:S(2)}) async-start(bf16[8,2,8]{2,1,0:T(2,128)(2,1)} %bitcast.1), calls=%async_computation.2 | async-start | bytes 8192 | tf_op jit(solution)/shard_map/all_to_all | solution.py:100
  15.6 1.0 reshape.145
  16.8 1.1 constant_dynamic-update-slice_fusion.5
  17.9 0.8 convolution_convert_fusion.10
  18.7 1.1 constant_dynamic-update-slice_fusion.4
  19.8 1.2 convolution_convert_fusion.7
  21.1 1.3 convolution_convert_fusion.6
  23.0 4.2 %all-to-all-start.1 = ((bf16[8,2,8]{2,1,0:T(2,128)(2,1)}), bf16[8,2,8]{2,1,0:T(2,128)(2,1)S(1)}, u32[]{:S(2)}, u32[]{:S(2)}) async-start(bf16[8,2,8]{2,1,0:T(2,128)(2,1)} %bitcast.2), calls=%async_computation.1 | async-start | bytes 8192 | tf_op jit(solution)/shard_map/all_to_all | solution.py:101
  27.2 0.8 all_to_all.28
  28.1 3.8 %all-to-all-done.1 = bf16[8,2,8]{2,1,0:T(2,128)(2,1)S(1)} async-done(((bf16[8,2,8]{2,1,0:T(2,128)(2,1)}), bf16[8,2,8]{2,1,0:T(2,128)(2,1)S(1)}, u32[]{:S(2)}, u32[]{:S(2)}) %all-to-all-start.1) | async-done | bytes 288 | tf_op jit(solution)/shard_map/all_to_all | solution.py:101
  31.9 3.4 %all-to-all-start = ((bf16[8,2,4096]{2,1,0:T(2,128)(2,1)}), bf16[8,2,4096]{2,1,0:T(2,128)(2,1)S(1)}, u32[]{:S(2)}, u32[]{:S(2)}) async-start(bf16[8,2,4096]{2,1,0:T(2,128)(2,1)} %all_to_all.28), calls=%async_computation | async-start | bytes 262144 | tf_op jit(solution)/shard_map/all_to_all | solution.py:99
  35.6 5.1 %all-to-all-done = bf16[8,2,4096]{2,1,0:T(2,128)(2,1)S(1)} async-done(((bf16[8,2,4096]{2,1,0:T(2,128)(2,1)}), bf16[8,2,4096]{2,1,0:T(2,128)(2,1)S(1)}, u32[]{:S(2)}, u32[]{:S(2)}) %all-to-all-start) | async-done | bytes 131104 | tf_op jit(solution)/shard_map/all_to_all | solution.py:99
  41.1 30.6 %while.17 = (s32[]{:T(128)}, bf16[4,512,128]{1,2,0:T(8,128)(2,1)}, bf16[4,512,128]{1,2,0:T(8,128)(2,1)}, bf16[4,128,128]{1,2,0:T(8,128)(2,1)}, bf16[4,128,128]{1...) while((s32[]{:T(128)}, bf16[4,512,128]{1,2,0:T(8,128)(2,1)}, ...), condition=%wide.region_5.6_spmd.clone, body=%wide.region_1.5_spmd.clone.sunk | while | flops 107726848 | bytes 13525743 | solution.py:64
  42.5 0.9 constant_dynamic-slice_fusion.9
  44.2 0.9 constant_dynamic-slice_fusion.10
  50.1 0.9 constant_dynamic-slice_fusion.9
  51.8 0.9 constant_dynamic-slice_fusion.10
  57.8 0.9 constant_dynamic-slice_fusion.9
  59.5 0.9 constant_dynamic-slice_fusion.10
  65.4 0.9 constant_dynamic-slice_fusion.9
  67.2 0.9 constant_dynamic-slice_fusion.10
  71.8 1.5 fusion.27
  74.0 0.8 copy-done.4
  75.5 1.9 %fusion.11 = bf16[2048,512]{1,0:T(8,128)(2,1)} fusion(f32[512,512]{1,0:T(8,128)S(1)} %fusion.27, f32[512,512]{1,0:T(8,128)S(1)} %get-tuple-element.169, f32[512,512]{1,0:T(8,128)S(1)} %get-tuple-element.168, f32[512,512]{1,0:T(8,128)S(1)} %convolution_bitcast_fusion), kind=kLoop, calls=%fused_computation.31 | loop fusion | flops 5242880 | bytes 6291456 | tf_op jit(solution)/shard_map/convert_element_type | solution.py:141
  78.6 3.4 %all-to-all-start.3 = ((bf16[8,2,4096]{2,1,0:T(2,128)(2,1)}), bf16[8,2,4096]{2,1,0:T(2,128)(2,1)S(1)}, u32[]{:S(2)}, u32[]{:S(2)}) async-start(bf16[8,2,4096]{2,1,0:T(2,128)(2,1)} %all_to_all.35), calls=%async_computation.3 | async-start | bytes 262144 | tf_op jit(solution)/shard_map/all_to_all | solution.py:127
  82.1 2.3 %convolution_convert_fusion.5 = bf16[512,512]{1,0:T(8,128)(2,1)} fusion(bf16[512,512]{0,1:T(8,128)(2,1)} %bitcast.123, bf16[512,512]{1,0:T(8,128)(2,1)S(1)} %copy-done.7), kind=kOutput, calls=%fused_computation.34 | convolution fusion | flops 268697600 | bytes 1572864 | tf_op jit(solution)/shard_map/dot_general | solution.py:119
  84.4 33.6 %reduce-scatter.2.cloned.1.call-done = bf16[256,512]{1,0:T(8,128)(2,1)} async-done(((bf16[2048,512]{1,0:T(8,128)(2,1)}), bf16[256,512]{1,0:T(8,128)(2,1)}) %reduce-scatter.2.cloned.1.call-update) | async-done | bytes 262160 | tf_op jit(solution)/shard_map/reduce_scatter | solution.py:141
  118.1 1.3 convolution_convert_fusion.4
  120.4 35.6 %all-reduce.2.cloned.1.call-done = bf16[256,512]{1,0:T(8,128)(2,1)} async-done(((bf16[256,512]{1,0:T(8,128)(2,1)}), bf16[256,512]{1,0:T(8,128)(2,1)}) %all-reduce.2.cloned.1.call-update) | async-done | bytes 262160 | tf_op jit(solution)/shard_map/psum | solution.py:142
  155.9 1.8 %convert_element_type.135 = f32[256,512]{1,0:T(8,128)} convert(bf16[256,512]{1,0:T(8,128)(2,1)} %all-reduce.2.cloned.1.call-done) | non-fusion elementwise | flops 131072 | bytes 786432 | tf_op jit(solution)/shard_map/convert_element_type | solution.py:142
  (129 shorter events, 27.4 us)
Async XLA Ops:
  7.2 13.9 %copy-start = (bf16[512,512]{1,0:T(8,128)(2,1)S(1)}, bf16[512,512]{1,0:T(8,128)(2,1)}, u32[]{:S(2)}) copy-start(bf16[512,512]{1,0:T(8,128)(2,1)} %param.21) | copy-start | bytes 1572868
  7.2 12.6 %copy-start.3 = (bf16[512,512]{1,0:T(8,128)(2,1)S(1)}, bf16[512,512]{1,0:T(8,128)(2,1)}, u32[]{:S(2)}) copy-start(bf16[512,512]{1,0:T(8,128)(2,1)} %param.12) | copy-start | bytes 1572868
  7.2 12.6 %copy-start.1 = (bf16[512,512]{1,0:T(8,128)(2,1)S(1)}, bf16[512,512]{1,0:T(8,128)(2,1)}, u32[]{:S(2)}) copy-start(bf16[512,512]{1,0:T(8,128)(2,1)} %param.17) | copy-start | bytes 1572868
  10.3 12.7 %all-to-all-start.2 = ((bf16[8,2,8]{2,1,0:T(2,128)(2,1)}), bf16[8,2,8]{2,1,0:T(2,128)(2,1)S(1)}, u32[]{:S(2)}, u32[]{:S(2)}) async-start(bf16[8,2,8]{2,1,0:T(2,128)(2,1)} %bitcast.1), calls=%async_computation.2 | async-start | bytes 8192 | tf_op jit(solution)/shard_map/all_to_all | solution.py:100
  15.6 5.5 %copy-start.6 = (bf16[512,512]{1,0:T(8,128)(2,1)S(1)}, bf16[512,512]{1,0:T(8,128)(2,1)}, u32[]{:S(2)}) copy-start(bf16[512,512]{1,0:T(8,128)(2,1)} %param.20) | copy-start | bytes 1572868
  23.0 8.9 %all-to-all-start.1 = ((bf16[8,2,8]{2,1,0:T(2,128)(2,1)}), bf16[8,2,8]{2,1,0:T(2,128)(2,1)S(1)}, u32[]{:S(2)}, u32[]{:S(2)}) async-start(bf16[8,2,8]{2,1,0:T(2,128)(2,1)} %bitcast.2), calls=%async_computation.1 | async-start | bytes 8192 | tf_op jit(solution)/shard_map/all_to_all | solution.py:101
  31.9 8.8 %all-to-all-start = ((bf16[8,2,4096]{2,1,0:T(2,128)(2,1)}), bf16[8,2,4096]{2,1,0:T(2,128)(2,1)S(1)}, u32[]{:S(2)}, u32[]{:S(2)}) async-start(bf16[8,2,4096]{2,1,0:T(2,128)(2,1)} %all_to_all.28), calls=%async_computation | async-start | bytes 262144 | tf_op jit(solution)/shard_map/all_to_all | solution.py:99
  35.3 82.8 %reduce-scatter.2.cloned.1.call-start = ((), (), s32[]{:S(2)}) async-start(), calls=%async_computation.5 | async-start | bytes 2359296 | tf_op jit(solution)/shard_map/reduce_scatter | solution.py:141
  71.8 1.5 copy-start.8
  71.8 1.5 copy-start.9
  73.8 1.0 copy-start.4
  73.8 1.2 copy-start.5
  77.4 4.7 %copy-start.7 = (bf16[512,512]{1,0:T(8,128)(2,1)S(1)}, bf16[512,512]{1,0:T(8,128)(2,1)}, u32[]{:S(2)}) copy-start(bf16[512,512]{1,0:T(8,128)(2,1)} %param.20) | copy-start | bytes 1572868
  77.4 40.7 %copy-start.2 = (bf16[512,512]{1,0:T(8,128)(2,1)S(1)}, bf16[512,512]{1,0:T(8,128)(2,1)}, u32[]{:S(2)}) copy-start(bf16[512,512]{1,0:T(8,128)(2,1)} %param.17) | copy-start | bytes 1572868
  78.6 40.7 %all-to-all-start.3 = ((bf16[8,2,4096]{2,1,0:T(2,128)(2,1)}), bf16[8,2,4096]{2,1,0:T(2,128)(2,1)S(1)}, u32[]{:S(2)}, u32[]{:S(2)}) async-start(bf16[8,2,4096]{2,1,0:T(2,128)(2,1)} %all_to_all.35), calls=%async_computation.3 | async-start | bytes 262144 | tf_op jit(solution)/shard_map/all_to_all | solution.py:127
  82.0 73.9 %all-reduce.2.cloned.1.call-start = ((), (), s32[]{:S(2)}) async-start(), calls=%async_computation.6 | async-start | bytes 524288 | tf_op jit(solution)/shard_map/psum | solution.py:142
Sparse Core Ops, SparseCore 0:
  77.5 40.4 reduce-scatter.1
  120.4 35.5 all-reduce.1
where the time goes:
time: 165 us
  waiting for transfers between devices  78.2 us (47%)
  local copies, waits for them, and re-layouts  26.2 us (16%)
  matrix products  19.5 us (12%)
  starting transfers between devices  16.2 us (10%)
  between operations  14.3 us (9%)
  other arithmetic  7.41 us (4%)
  loops' own time  2.68 us (2%)
    psum x1, waiting for transfers between devices, per_device(): grads = lax.psum(band_rows, 'grp').astype(jnp.float32)  35.6 us
    reduce_scatter x1, waiting for transfers between devices, per_device(): lax.psum_scatter(term.astype(jnp.bfloat16), 'band', scatter_dimension=0,...  33.6 us
    dynamic_update_slice x8, local copies, waits for them, and re-layouts, band_attention(): stacked = lax.map(per_group, jnp.arange(groups))  5.51 us
    all_to_all x1, starting transfers between devices, per_device(): lax.all_to_all(send_bias, 'band', split_axis=0, concat_axis=0, tiled=True)  5.2 us
    all_to_all x1, waiting for transfers between devices, per_device(): lax.all_to_all(send_feat, 'band', split_axis=0, concat_axis=0, tiled=True)  5.13 us
    all_to_all x1, starting transfers between devices, per_device(): lax.all_to_all(send_mask, 'band', split_axis=0, concat_axis=0, tiled=True)  4.19 us
    dynamic_slice x8, local copies, waits for them, and re-layouts, per_group(): lax.dynamic_slice_in_dim(query, start, group_width, 1)  4.14 us
    dynamic_slice x8, local copies, waits for them, and re-layouts, per_group(): lax.dynamic_slice_in_dim(dattn, start, group_width, 1)  4.14 us
  transfers between devices with their start and end apart: 6, of which 4 were waited for; matrix products, arithmetic and copies ran while one was open for 8% of the time, Pallas kernels for 0%

commit v1 on v0

v1 whole, which is shorter than its diff:
```python
import functools
import math

import jax
import jax.numpy as jnp
from jax import lax
from jax.experimental import pallas as pl
from jax.experimental.pallas import tpu as pltpu
from jax.sharding import PartitionSpec as P

HEADS = 16
CAP = 2
F32 = jnp.float32
BF16 = jnp.bfloat16
MESH = pl.DeviceIdType.MESH
HIDDEN = -1e30
LANES = 128


def mm(a, b):
    return lax.dot_general(a, b, (((1,), (0,)), ((), ())), preferred_element_type=F32)


def mm_nt(a, b):
    return lax.dot_general(a, b, (((1,), (1,)), ((), ())), preferred_element_type=F32)


def mm_tn(a, b):
    return lax.dot_general(a, b, (((0,), (0,)), ((), ())), preferred_element_type=F32)


def iota(shape, axis):
    return lax.broadcasted_iota(jnp.int32, shape, axis)


def kernel(
    n,
    g,
    latent,
    feat,
    bias,
    route,
    tmask,
    wq,
    wk,
    wv,
    wo,
    gout,
    attended,
    grad_latent,
    grad_obs,
    grads,
    sbuf,
    rbuf,
    place,
    addt,
    q_s,
    qt_s,
    da_s,
    dat_s,
    k_s,
    v_s,
    kt_s,
    vt_s,
    attnt_s,
    dqt_s,
    dk_s,
    dv_s,
    dq_s,
    attn_s,
    fsend,
    frecv,
    a2a_ss,
    a2a_rs,
    ret_ss,
    ret_rs,
    rs_ss,
    rs_rs,
    z_ss,
    z_rs,
    zg_ss,
    zg_rs,
    *rest,
):
    me = lax.axis_index("band")
    mz = lax.axis_index("grp")
    lat_rows, width = latent.shape
    obs_rows = feat.shape[0]
    blocks, tiles = tmask.shape
    ob = obs_rows // blocks
    key_rows = n * CAP * ob
    part = CAP * ob
    head = width // HEADS
    scale = 1.0 / math.sqrt(head)
    chunks = width // LANES
    levels = n.bit_length() - 1
    rows = 4 * width // n
    zrows = rows // g
    two_step = zrows % 16 == 0

    term = rest[:chunks]
    pos_at = chunks
    recv = []
    acc = []
    for c in range(chunks):
        recv.append(rest[pos_at : pos_at + levels])
        pos_at += levels
        acc.append(rest[pos_at : pos_at + levels])
        pos_at += levels
    zrecv, zown, zfull = rest[pos_at : pos_at + 3]

    barrier = pltpu.get_barrier_semaphore()
    for d in range(1, n):
        pl.semaphore_signal(
            barrier, inc=1, device_id={"band": lax.rem(me + d, n)}, device_id_type=MESH
        )
    for d in range(1, g):
        pl.semaphore_signal(
            barrier, inc=1, device_id={"grp": lax.rem(mz + d, g)}, device_id_type=MESH
        )

    blk_of = iota((blocks, obs_rows), 1) // ob
    row_id = iota((blocks, obs_rows), 0)
    expand = blk_of == row_id
    route_c = jnp.broadcast_to(route[...], (blocks, obs_rows))
    route_r = jnp.sum(jnp.where(expand, route_c, 0), axis=0, keepdims=True)
    rank_r = jnp.sum(
        jnp.where((route_c == route_r) & (row_id < blk_of), 1, 0), axis=0, keepdims=True
    )
    dest = (route_r * CAP + rank_r) * ob + lax.rem(iota((1, obs_rows), 1), ob)
    hit = iota((key_rows, obs_rows), 0) == dest
    placing = jnp.where(hit, 1.0, 0.0).astype(BF16)
    place[...] = placing
    sbuf[:, :, :width] = mm(placing, feat[...]).astype(BF16).reshape(n, part, width)
    widen = jnp.where(iota((tiles, LANES), 0) == iota((tiles, LANES), 1), 1.0, 0.0).astype(BF16)
    mask_w = mm(tmask[...].astype(F32).astype(BF16), widen).astype(BF16)
    mask_o = mm_tn(jnp.where(expand, 1.0, 0.0).astype(BF16), mask_w).astype(BF16)
    bias_col = jnp.sum(jnp.where(hit, bias[...].astype(F32), 0.0), axis=1, keepdims=True)
    meta_s = mm(placing, mask_o) + jnp.where(iota((key_rows, LANES), 1) == tiles, bias_col, 0.0)
    sbuf[:, :, width:] = meta_s.astype(BF16).reshape(n, part, LANES)

    pl.semaphore_wait(barrier, n - 1 + g - 1)

    def exchange(src, dst, ss, rs):
        copies = []
        for d in range(1, n):
            peer = lax.rem(me + d, n)
            copy = pltpu.make_async_remote_copy(
                src_ref=src.at[peer],
                dst_ref=dst.at[me],
                send_sem=ss.at[d],
                recv_sem=rs.at[d],
                device_id={"band": peer},
                device_id_type=MESH,
            )
            copy.start()
            copies.append(copy)
        return copies

    a2a = exchange(sbuf, rbuf, a2a_ss, a2a_rs)
    rbuf[me] = sbuf[me]

    query = mm(latent[...], wq[...]).astype(BF16)
    q_s[...] = query
    qt_s[...] = query.T
    dattn = mm_nt(gout[...], wo[...]).astype(BF16)
    da_s[...] = dattn
    dat_s[...] = dattn.T
    dk_s[...] = jnp.zeros_like(dk_s)
    dv_s[...] = jnp.zeros_like(dv_s)

    for copy in a2a:
        copy.wait()
    got = rbuf[:, :, :width].reshape(key_rows, width)
    keys = mm(got, wk[...]).astype(BF16)
    values = mm(got, wv[...]).astype(BF16)
    k_s[...] = keys
    v_s[...] = values
    kt_s[...] = keys.T
    vt_s[...] = values.T
    meta = rbuf[:, :, width:].reshape(key_rows, LANES)
    pick = jnp.where(
        iota((LANES, lat_rows), 0) == iota((LANES, lat_rows), 1) // (lat_rows // tiles), 1.0, 0.0
    ).astype(BF16)
    bias_pick = jnp.where(iota((LANES, lat_rows), 0) == tiles, 1.0, 0.0).astype(BF16)
    addt[...] = jnp.where(mm(meta, pick) > 0.5, mm(meta, bias_pick), HIDDEN)

    gw = min(256, width)
    per_group = gw // head
    unroll = 2
    for grp_at in range(width // gw):
        cols = slice(grp_at * gw, (grp_at + 1) * gw)

        def one_head(local):
            lane_head = iota((1, gw), 1) // head
            own = jnp.where(lane_head == local, 1.0, 0.0)
            own_b = own.astype(BF16)
            start = pl.multiple_of(grp_at * gw + local * head, head)
            hrows = pl.ds(start, head)
            scores = mm(k_s[:, cols] * own_b, qt_s[cols, :]) * scale + addt[...]
            top = jnp.maximum(jnp.max(scores, axis=0, keepdims=True), 0.0)
            expo = jnp.exp(scores - top)
            total = jnp.exp(-top) + jnp.sum(expo, axis=0, keepdims=True)
            prob = expo * (1.0 / total)
            prob_b = prob.astype(BF16)
            attnt_s[hrows, :] = mm(vt_s[hrows, :], prob_b).astype(BF16)
            dprob = mm(v_s[:, cols] * own_b, dat_s[cols, :])
            delta = jnp.sum(prob * dprob, axis=0, keepdims=True)
            dscore = (prob * (dprob - delta)).astype(BF16)
            dqt_s[hrows, :] = (mm(kt_s[hrows, :], dscore) * scale).astype(BF16)
            dk_s[:, cols] += mm(dscore, q_s[:, cols]) * own
            dv_s[:, cols] += mm(prob_b, da_s[:, cols]) * own

        def pair(i, carry):
            for u in range(unroll):
                one_head(i * unroll + u)
            return carry

        lax.fori_loop(0, per_group // unroll, pair, 0)

    dkeys = (dk_s[...] * scale).astype(BF16)
    dvalues = dv_s[...].astype(BF16)
    fsend[...] = (
        (mm_nt(dkeys, wk[...]) + mm_nt(dvalues, wv[...])).astype(BF16).reshape(n, part, width)
    )
    ret = exchange(fsend, frecv, ret_ss, ret_rs)
    frecv[me] = fsend[me]

    dq_s[...] = dqt_s[...].T
    share = 1.0 / float(g)

    started = []

    def low_first(c, level):
        return level == 0 or c % 2 == 0

    def bit_of(c, level):
        if level == 0 or c % 2 == 0:
            return level
        return levels - level

    def source(c, level):
        return term[c] if level == 0 else acc[c][level - 1]

    def side(c, level, which):
        ref = source(c, level)
        if low_first(c, level):
            return ref.at[:, which]
        return ref.at[which]

    def level_copy(c, level):
        step = 1 << bit_of(c, level)
        mine = lax.rem(me // step, 2)
        partner = me + (1 - 2 * mine) * step
        return mine, pltpu.make_async_remote_copy(
            src_ref=side(c, level, 1 - mine),
            dst_ref=recv[c][level],
            send_sem=rs_ss.at[c, level],
            recv_sem=rs_rs.at[c, level],
            device_id={"band": partner},
            device_id_type=MESH,
        )

    def start_level(c, level):
        copy = level_copy(c, level)[1]
        copy.start()
        started.append(copy)

    def finish_level(c, level):
        mine, copy = level_copy(c, level)
        copy.wait_recv()
        total = (side(c, level, mine)[...].astype(F32) + recv[c][level][...].astype(F32)).astype(
            BF16
        )
        if level == levels - 1 and not two_step:
            acc[c][level][...] = total.reshape(rows, LANES)
        else:
            acc[c][level][...] = total.reshape(acc[c][level].shape)

    def z_copies(c):
        copies = []
        for d in range(1, g):
            peer = lax.rem(mz + d, g)
            full = acc[c][levels - 1]
            copies.append(
                pltpu.make_async_remote_copy(
                    src_ref=full.at[peer] if two_step else full,
                    dst_ref=zrecv.at[c, d],
                    send_sem=z_ss.at[c, d],
                    recv_sem=z_rs.at[c, d],
                    device_id={"grp": peer},
                    device_id_type=MESH,
                )
            )
        return copies

    def zg_copies(c):
        copies = []
        for d in range(1, g):
            peer = lax.rem(mz + d, g)
            copies.append(
                pltpu.make_async_remote_copy(
                    src_ref=zown.at[c],
                    dst_ref=zfull.at[c, mz],
                    send_sem=zg_ss.at[c, d],
                    recv_sem=zg_rs.at[c, d],
                    device_id={"grp": peer},
                    device_id_type=MESH,
                )
            )
        return copies

    def begin(copies):
        for copy in copies:
            copy.start()
            started.append(copy)

    def z_total(c):
        for copy in z_copies(c):
            copy.wait_recv()
        full = acc[c][levels - 1]
        total = (full[mz] if two_step else full[...]).astype(F32)
        for d in range(1, g):
            total = total + zrecv[c, d].astype(F32)
        return total

    def out_cols(c):
        return slice(c * LANES, (c + 1) * LANES)

    def event(c, level):
        if level < levels:
            finish_level(c, level)
            if level + 1 < levels:
                start_level(c, level + 1)
            else:
                begin(z_copies(c))
        elif level == levels:
            total = z_total(c)
            if two_step:
                zown[c] = total.astype(BF16)
                begin(zg_copies(c))
                zfull[c, mz] = total.astype(BF16)
            else:
                grads[:, out_cols(c)] = total
        elif two_step:
            for copy in zg_copies(c):
                copy.wait_recv()
            grads[:, out_cols(c)] = zfull[c].reshape(rows, LANES).astype(F32)

    got2 = rbuf[:, :, :width].reshape(key_rows, width)
    wave = 2
    waves = chunks // wave
    for p in range(waves):
        cols = slice(p * wave * LANES, (p + 1) * wave * LANES)
        pieces = (
            mm_tn(latent[...], dq_s[:, cols]),
            mm_tn(got2, dkeys[:, cols]),
            mm_tn(got2, dvalues[:, cols]),
            mm(attnt_s[...], gout[:, cols]),
        )
        for u in range(wave):
            c = p * wave + u
            for w, piece in enumerate(pieces):
                value = (piece[:, u * LANES : (u + 1) * LANES] * share).astype(BF16)
                term[c][w * n // 8 : (w + 1) * n // 8] = value.reshape(n // 8, 2, rows, LANES)
            start_level(c, 0)

    attn_s[...] = attnt_s[...].T
    steps = levels + 2
    for t in range(steps + waves - 1):
        for p in range(waves):
            level = t - p
            if 0 <= level < steps:
                for u in range(wave):
                    event(p * wave + u, level)
        if t == 0:
            grad_latent[...] = mm_nt(dq_s[...], wq[...]).astype(BF16)
        if t == 1:
            attended[...] = mm(attn_s[...], wo[...]).astype(BF16)
        if t == 2:
            for copy in ret:
                copy.wait()
            grad_obs[...] = mm_tn(place[...], frecv[...].reshape(key_rows, width)).astype(BF16)
    for copy in started:
        copy.wait_send()


def per_device(n, g, *args):
    latent, feat, bias, route, tmask, wq, wk, wv, wo, gout = args
    lat_rows, width = latent.shape
    obs_rows = feat.shape[0]
    blocks = route.shape[0]
    part = CAP * (obs_rows // blocks)
    key_rows = n * part
    chunks = width // LANES
    levels = n.bit_length() - 1
    rows = 4 * width // n
    two_step = (rows // g) % 16 == 0
    vm = pltpu.VMEM
    sem = pltpu.SemaphoreType.DMA
    scratch = [
        vm((n, part, width + LANES), BF16),
        vm((n, part, width + LANES), BF16),
        vm((key_rows, obs_rows), BF16),
        vm((key_rows, lat_rows), F32),
        vm((lat_rows, width), BF16),
        vm((width, lat_rows), BF16),
        vm((lat_rows, width), BF16),
        vm((width, lat_rows), BF16),
        vm((key_rows, width), BF16),
        vm((key_rows, width), BF16),
        vm((width, key_rows), BF16),
        vm((width, key_rows), BF16),
        vm((width, lat_rows), BF16),
        vm((width, lat_rows), BF16),
        vm((key_rows, width), F32),
        vm((key_rows, width), F32),
        vm((lat_rows, width), BF16),
        vm((lat_rows, width), BF16),
        vm((n, part, width), BF16),
        vm((n, part, width), BF16),
        sem((n,)),
        sem((n,)),
        sem((n,)),
        sem((n,)),
        sem((chunks, levels)),
        sem((chunks, levels)),
        sem((chunks, g)),
        sem((chunks, g)),
        sem((chunks, g)),
        sem((chunks, g)),
    ]
    scratch += [vm((n // 2, 2, rows, LANES), BF16) for _ in range(chunks)]
    for c in range(chunks):
        for level in range(levels):
            scratch.append(vm((n >> (level + 1), rows, LANES), BF16))
        for level in range(levels):
            m = n >> (level + 1)
            if level == levels - 1:
                shape = (g, rows // g, LANES) if two_step else (rows, LANES)
            elif c % 2 == 0:
                shape = (m // 2, 2, rows, LANES)
            else:
                shape = (2, m // 2, rows, LANES)
            scratch.append(vm(shape, BF16))
    zr = rows // g if two_step else rows
    scratch.append(vm((chunks, g, zr, LANES), BF16))
    scratch.append(vm((chunks, zr, LANES), BF16))
    scratch.append(vm((chunks, g, zr, LANES), BF16))
    spec = pl.BlockSpec(memory_space=pltpu.VMEM)
    return pl.pallas_call(
        functools.partial(kernel, n, g),
        out_shape=(
            jax.ShapeDtypeStruct((lat_rows, width), BF16),
            jax.ShapeDtypeStruct((lat_rows, width), BF16),
            jax.ShapeDtypeStruct((obs_rows, width), BF16),
            jax.ShapeDtypeStruct((rows, width), F32),
        ),
        in_specs=[spec] * 10,
        out_specs=(spec,) * 4,
        scratch_shapes=scratch,
        compiler_params=pltpu.CompilerParams(
            collective_id=0, has_side_effects=True, vmem_limit_bytes=60 * 1024 * 1024
        ),
        name="fused_layer",
    )(latent, feat, bias.reshape(1, obs_rows), route, tmask, wq, wk, wv, wo, gout)


def solution(mesh):
    n = mesh.shape["band"]
    g = mesh.shape["grp"]
    return jax.shard_map(
        functools.partial(per_device, n, g),
        mesh=mesh,
        in_specs=(
            P(("grp", "band"), None),
            P(("grp", "band"), None),
            P(("grp", "band")),
            P(("grp", "band"), None),
            P(("grp", "band"), None),
            P(),
            P(),
            P(),
            P(),
            P(("grp", "band"), None),
        ),
        out_specs=(
            P(("grp", "band"), None),
            P(("grp", "band"), None),
            P(("grp", "band"), None),
            P("band", None),
        ),
        check_vma=False,
    )
```

time: 165 us -> 58.6 us (0.36)
  waiting for transfers between devices: 78.2 us -> 0 us
  Pallas kernels: 0 us -> 51.3 us
  local copies, waits for them, and re-layouts: 26.2 us -> 6.38 us
  matrix products: 19.5 us -> 0 us
  starting transfers between devices: 16.2 us -> 0 us
  between operations: 14.3 us -> 0.66 us
  other arithmetic: 7.41 us -> 0 us
  loops' own time: 2.68 us -> 0 us
    pallas_call x0 -> x1, Pallas kernels: none -> 51.3 us  [per_device(): pl.pallas_call(functools.partial(kernel, n, g), out_shape=(jax.ShapeDtype...]
    psum x1 -> x0, waiting for transfers between devices: 35.6 us -> none  [per_device(): grads = lax.psum(band_rows, 'grp').astype(jnp.float32)]
    reduce_scatter x1 -> x0, waiting for transfers between devices: 33.6 us -> none  [per_device(): lax.psum_scatter(term.astype(jnp.bfloat16), 'band', scatter_dimension=0,...]
    dot_general x38 -> x0, matrix products: 19.5 us -> none  [the longest x1 2.31 us: per_device(): jnp.dot(attn, w_out, preferred_element_type=jnp.float32)]
    all_to_all x4 -> x0, starting transfers between devices: 16.1 us -> none  [the longest x1 5.2 us: per_device(): lax.all_to_all(send_bias, 'band', split_axis=0, concat_axis=0, tiled=True)]
    dynamic_slice x36 -> x0, local copies, waits for them, and re-layouts: 11.6 us -> none  [the longest x8 4.14 us: per_group(): lax.dynamic_slice_in_dim(query, start, group_width, 1)]
    all_to_all x4 -> x0, waiting for transfers between devices: 8.98 us -> none  [the longest x1 5.13 us: per_device(): lax.all_to_all(send_feat, 'band', split_axis=0, concat_axis=0, tiled=True)]
    dynamic_update_slice x8 -> x0, local copies, waits for them, and re-layouts: 5.51 us -> none  [band_attention(): stacked = lax.map(per_group, jnp.arange(groups))]
  transfers between devices with their start and end apart: 6 -> 0, of which waited for: 4 -> 0; matrix products, arithmetic and copies ran while one was open for 8% -> 0% of each run, Pallas kernels for 0% -> 0%
where the time goes in v1:
time: 58.6 us; the launch traced here: 58.4 us
  Pallas kernels  51.3 us (88%)
  local copies, waits for them, and re-layouts  6.38 us (11%)
  between operations  0.66 us (1%)
    pallas_call x1, Pallas kernels, per_device(): pl.pallas_call(functools.partial(kernel, n, g), out_shape=(jax.ShapeDtype...  51.3 us
    unnamed x16, local copies, waits for them, and re-layouts  6.38 us

profile of v1, /device:TPU:0, one launch (start us, length us, event | category | flops | bytes accessed | tf_op | source)
XLA Modules:
  0.0 58.4 jit_solution(447774315473356228)
XLA Ops:
  0.6 0.0 copy-start.4
  0.6 0.6 %copy-done.4 = s32[16,1]{0,1:T(1,128)S(1)} copy-done((s32[16,1]{0,1:T(1,128)S(1)}, s32[16,1]{0,1:T(1,128)}, u32[]{:S(2)}) %copy-start.4) | copy-done | bytes 88
  1.3 0.0 copy-start.3
  1.3 0.7 %copy.14.route = s32[16,1]{1,0:T(8,128)} copy(s32[16,1]{0,1:T(1,128)S(1)} %copy-done.4) | data formatting | bytes 128 | tf_op args[3]
  2.0 0.0 copy-done.3
  2.0 0.7 %copy.15.tmask = s32[16,8]{1,0:T(8,128)} copy(s32[16,8]{0,1:T(8,128)S(1)} %copy-done.3) | data formatting | bytes 1024 | tf_op args[4]
  2.6 51.3 %fused_layer.1 = (bf16[512,512]{1,0:T(8,128)(2,1)}, bf16[512,512]{1,0:T(8,128)(2,1)}, bf16[128,512]{1,0:T(8,128)(2,1)}, f32[256,512]{1,0:T(8,128)}) custom-call(bf16[512,512]{1,0:T(8,128)(2,1)} %latent.1, bf16[128,512]{1,0:T(8,128)(2,1)} %feat.1, bf16[1,128]{1,0:T(2,128)(2,1)} %bitcast.1, s32[16,1]{1,0:T(8,128)} %copy.14.route, s32[16,8]{1,0:T(8,128)} %copy.15.tmask, ...), custom_call_target="tpu_custom_call" | custom-call | tf_op jit(solution)/shard_map/fused_layer/pallas_call | solution.py:451
  54.0 0.0 copy-start.1
  54.0 1.9 %copy.20 = bf16[512,512]{1,0:T(8,128)(2,1)} copy(bf16[512,512]{1,0:T(8,128)(2,1)} %get-tuple-element.8) | data formatting | bytes 1048576
  55.9 0.0 copy-done.1
  55.9 0.0 copy-start.2
  55.9 0.0 copy-start
  55.9 0.8 %copy.21 = bf16[512,512]{1,0:T(8,128)(2,1)} copy(bf16[512,512]{1,0:T(8,128)(2,1)S(1)} %copy-done.1) | data formatting | bytes 1048576
  56.7 0.2 copy-done.2
  56.9 0.7 %copy.22 = bf16[128,512]{1,0:T(8,128)(2,1)} copy(bf16[128,512]{1,0:T(8,128)(2,1)S(1)} %copy-done.2) | data formatting | bytes 262144
  57.6 0.0 copy-done
  57.6 0.8 %copy.23 = f32[256,512]{1,0:T(8,128)} copy(f32[256,512]{1,0:T(8,128)S(1)} %copy-done) | data formatting | bytes 1048576
Async XLA Ops:
  0.6 0.7 %copy-start.4 = (s32[16,1]{0,1:T(1,128)S(1)}, s32[16,1]{0,1:T(1,128)}, u32[]{:S(2)}) copy-start(s32[16,1]{0,1:T(1,128)} %param.13) | copy-start | bytes 196
  1.3 0.7 %copy-start.3 = (s32[16,8]{0,1:T(8,128)S(1)}, s32[16,8]{0,1:T(8,128)}, u32[]{:S(2)}) copy-start(s32[16,8]{0,1:T(8,128)} %param.14) | copy-start | bytes 1540
  54.0 1.9 %copy-start.1 = (bf16[512,512]{1,0:T(8,128)(2,1)S(1)}, bf16[512,512]{1,0:T(8,128)(2,1)}, u32[]{:S(2)}) copy-start(bf16[512,512]{1,0:T(8,128)(2,1)} %get-tuple-element.9) | copy-start | bytes 1572868
  55.9 1.0 %copy-start.2 = (bf16[128,512]{1,0:T(8,128)(2,1)S(1)}, bf16[128,512]{1,0:T(8,128)(2,1)}, u32[]{:S(2)}) copy-start(bf16[128,512]{1,0:T(8,128)(2,1)} %get-tuple-element.10) | copy-start | bytes 393220
  55.9 1.7 %copy-start = (f32[256,512]{1,0:T(8,128)S(1)}, f32[256,512]{1,0:T(8,128)}, u32[]{:S(2)}) copy-start(f32[256,512]{1,0:T(8,128)} %get-tuple-element.11) | copy-start | bytes 1572868

commit v2 on v1

--- a/solution.py
+++ b/solution.py
@@ -36,20 +36,31 @@
 def kernel(
     n,
     g,
-    latent,
-    feat,
+    latent_h,
+    feat_h,
     bias,
     route,
     tmask,
+    wq_h,
+    wk_h,
+    wv_h,
+    wo_h,
+    gout_h,
+    attended,
+    grad_latent,
+    grad_obs,
+    grads,
+    latent,
+    feat,
     wq,
     wk,
     wv,
     wo,
     gout,
-    attended,
-    grad_latent,
-    grad_obs,
-    grads,
+    in_sem,
+    latt_s,
+    gott_s,
+    prob_s,
     sbuf,
     rbuf,
     place,
@@ -86,7 +97,7 @@
     mz = lax.axis_index("grp")
     lat_rows, width = latent.shape
     obs_rows = feat.shape[0]
-    blocks, tiles = tmask.shape
+    tiles, blocks = tmask.shape
     ob = obs_rows // blocks
     key_rows = n * CAP * ob
     part = CAP * ob
@@ -109,6 +120,18 @@
         pos_at += levels
     zrecv, zown, zfull = rest[pos_at : pos_at + 3]
 
+    pairs = (
+        (feat_h, feat),
+        (latent_h, latent),
+        (wq_h, wq),
+        (gout_h, gout),
+        (wo_h, wo),
+        (wk_h, wk),
+        (wv_h, wv),
+    )
+    loads = [pltpu.make_async_copy(a, b, in_sem.at[i]) for i, (a, b) in enumerate(pairs)]
+    for load in loads:
+        load.start()
     barrier = pltpu.get_barrier_semaphore()
     for d in range(1, n):
         pl.semaphore_signal(
@@ -122,7 +145,10 @@
     blk_of = iota((blocks, obs_rows), 1) // ob
     row_id = iota((blocks, obs_rows), 0)
     expand = blk_of == row_id
-    route_c = jnp.broadcast_to(route[...], (blocks, obs_rows))
+    expand_b = jnp.where(expand, 1.0, 0.0).astype(BF16)
+    diagonal = iota((blocks, blocks), 0) == iota((blocks, blocks), 1)
+    route_d = jnp.where(diagonal, route[...].astype(F32), 0.0).astype(BF16)
+    route_c = mm(route_d, jnp.ones((blocks, obs_rows), BF16)).astype(jnp.int32)
     route_r = jnp.sum(jnp.where(expand, route_c, 0), axis=0, keepdims=True)
     rank_r = jnp.sum(
         jnp.where((route_c == route_r) & (row_id < blk_of), 1, 0), axis=0, keepdims=True
@@ -131,10 +157,11 @@
     hit = iota((key_rows, obs_rows), 0) == dest
     placing = jnp.where(hit, 1.0, 0.0).astype(BF16)
     place[...] = placing
+    loads[0].wait()
     sbuf[:, :, :width] = mm(placing, feat[...]).astype(BF16).reshape(n, part, width)
     widen = jnp.where(iota((tiles, LANES), 0) == iota((tiles, LANES), 1), 1.0, 0.0).astype(BF16)
-    mask_w = mm(tmask[...].astype(F32).astype(BF16), widen).astype(BF16)
-    mask_o = mm_tn(jnp.where(expand, 1.0, 0.0).astype(BF16), mask_w).astype(BF16)
+    mask_w = mm_tn(tmask[...].astype(F32).astype(BF16), widen).astype(BF16)
+    mask_o = mm_tn(expand_b, mask_w).astype(BF16)
     bias_col = jnp.sum(jnp.where(hit, bias[...].astype(F32), 0.0), axis=1, keepdims=True)
     meta_s = mm(placing, mask_o) + jnp.where(iota((key_rows, LANES), 1) == tiles, bias_col, 0.0)
     sbuf[:, :, width:] = meta_s.astype(BF16).reshape(n, part, LANES)
@@ -160,18 +187,26 @@
     a2a = exchange(sbuf, rbuf, a2a_ss, a2a_rs)
     rbuf[me] = sbuf[me]
 
+    loads[1].wait()
+    loads[2].wait()
     query = mm(latent[...], wq[...]).astype(BF16)
     q_s[...] = query
     qt_s[...] = query.T
+    loads[3].wait()
+    loads[4].wait()
     dattn = mm_nt(gout[...], wo[...]).astype(BF16)
     da_s[...] = dattn
     dat_s[...] = dattn.T
+    latt_s[...] = latent[...].T
     dk_s[...] = jnp.zeros_like(dk_s)
     dv_s[...] = jnp.zeros_like(dv_s)
 
+    loads[5].wait()
+    loads[6].wait()
     for copy in a2a:
         copy.wait()
     got = rbuf[:, :, :width].reshape(key_rows, width)
+    gott_s[...] = got.T
     keys = mm(got, wk[...]).astype(BF16)
     values = mm(got, wv[...]).astype(BF16)
     k_s[...] = keys
@@ -188,45 +223,55 @@
     gw = min(256, width)
     per_group = gw // head
     unroll = 2
+    heads_per_chunk = LANES // head
+
+    def place_of(grp_at, local):
+        own = jnp.where(iota((1, gw), 1) // head == local, 1.0, 0.0)
+        start = pl.multiple_of(grp_at * gw + local * head, head)
+        return own, pl.ds(start, head)
+
     for grp_at in range(width // gw):
-        cols = slice(grp_at * gw, (grp_at + 1) * gw)
-
-        def one_head(local):
-            lane_head = iota((1, gw), 1) // head
-            own = jnp.where(lane_head == local, 1.0, 0.0)
-            own_b = own.astype(BF16)
-            start = pl.multiple_of(grp_at * gw + local * head, head)
-            hrows = pl.ds(start, head)
-            scores = mm(k_s[:, cols] * own_b, qt_s[cols, :]) * scale + addt[...]
+
+        def forward(local, grp_at=grp_at):
+            cols = slice(grp_at * gw, (grp_at + 1) * gw)
+            own, hrows = place_of(grp_at, local)
+            scores = mm(k_s[:, cols] * own.astype(BF16), qt_s[cols, :]) * scale + addt[...]
             top = jnp.maximum(jnp.max(scores, axis=0, keepdims=True), 0.0)
             expo = jnp.exp(scores - top)
             total = jnp.exp(-top) + jnp.sum(expo, axis=0, keepdims=True)
             prob = expo * (1.0 / total)
-            prob_b = prob.astype(BF16)
-            attnt_s[hrows, :] = mm(vt_s[hrows, :], prob_b).astype(BF16)
-            dprob = mm(v_s[:, cols] * own_b, dat_s[cols, :])
-            delta = jnp.sum(prob * dprob, axis=0, keepdims=True)
-            dscore = (prob * (dprob - delta)).astype(BF16)
-            dqt_s[hrows, :] = (mm(kt_s[hrows, :], dscore) * scale).astype(BF16)
-            dk_s[:, cols] += mm(dscore, q_s[:, cols]) * own
-            dv_s[:, cols] += mm(prob_b, da_s[:, cols]) * own
-
-        def pair(i, carry):
+            prob_s[grp_at * per_group + local] = prob
+            attnt_s[hrows, :] = mm(vt_s[hrows, :], prob.astype(BF16)).astype(BF16)
+
+        def forwards(i, carry, forward=forward):
             for u in range(unroll):
-                one_head(i * unroll + u)
+                forward(i * unroll + u)
             return carry
 
-        lax.fori_loop(0, per_group // unroll, pair, 0)
-
-    dkeys = (dk_s[...] * scale).astype(BF16)
-    dvalues = dv_s[...].astype(BF16)
-    fsend[...] = (
-        (mm_nt(dkeys, wk[...]) + mm_nt(dvalues, wv[...])).astype(BF16).reshape(n, part, width)
-    )
-    ret = exchange(fsend, frecv, ret_ss, ret_rs)
-    frecv[me] = fsend[me]
-
-    dq_s[...] = dqt_s[...].T
+        lax.fori_loop(0, per_group // unroll, forwards, 0)
+
+    def backward(grp_at, local):
+        cols = slice(grp_at * gw, (grp_at + 1) * gw)
+        own, hrows = place_of(grp_at, local)
+        prob = prob_s[grp_at * per_group + local]
+        dprob = mm(v_s[:, cols] * own.astype(BF16), dat_s[cols, :])
+        delta = jnp.sum(prob * dprob, axis=0, keepdims=True)
+        dscore = (prob * (dprob - delta)).astype(BF16)
+        dqt_s[hrows, :] = (mm(kt_s[hrows, :], dscore) * scale).astype(BF16)
+        dk_s[:, cols] += mm(dscore, q_s[:, cols]) * own
+        dv_s[:, cols] += mm(prob.astype(BF16), da_s[:, cols]) * own
+
+    def backward_chunk(c):
+        grp_at = c * LANES // gw
+        first = (c * LANES - grp_at * gw) // head
+
+        def backwards(i, carry):
+            for u in range(unroll):
+                backward(grp_at, first + i * unroll + u)
+            return carry
+
+        lax.fori_loop(0, heads_per_chunk // unroll, backwards, 0)
+
     share = 1.0 / float(g)
 
     started = []
@@ -347,37 +392,46 @@
                 copy.wait_recv()
             grads[:, out_cols(c)] = zfull[c].reshape(rows, LANES).astype(F32)
 
-    got2 = rbuf[:, :, :width].reshape(key_rows, width)
-    wave = 2
-    waves = chunks // wave
-    for p in range(waves):
-        cols = slice(p * wave * LANES, (p + 1) * wave * LANES)
+    steps = levels + 2
+
+    def events(t):
+        for c in range(chunks):
+            level = t - c - 1
+            if 0 <= level < steps:
+                event(c, level)
+
+    for c in range(chunks):
+        backward_chunk(c)
+        cols = out_cols(c)
+        dq = dqt_s[cols, :].T
+        dq_s[:, cols] = dq
         pieces = (
-            mm_tn(latent[...], dq_s[:, cols]),
-            mm_tn(got2, dkeys[:, cols]),
-            mm_tn(got2, dvalues[:, cols]),
+            mm(latt_s[...], dq),
+            mm(gott_s[...], (dk_s[:, cols] * scale).astype(BF16)),
+            mm(gott_s[...], dv_s[:, cols].astype(BF16)),
             mm(attnt_s[...], gout[:, cols]),
         )
-        for u in range(wave):
-            c = p * wave + u
-            for w, piece in enumerate(pieces):
-                value = (piece[:, u * LANES : (u + 1) * LANES] * share).astype(BF16)
-                term[c][w * n // 8 : (w + 1) * n // 8] = value.reshape(n // 8, 2, rows, LANES)
-            start_level(c, 0)
-
-    attn_s[...] = attnt_s[...].T
-    steps = levels + 2
-    for t in range(steps + waves - 1):
-        for p in range(waves):
-            level = t - p
-            if 0 <= level < steps:
-                for u in range(wave):
-                    event(p * wave + u, level)
-        if t == 0:
+        for w, piece in enumerate(pieces):
+            value = (piece * share).astype(BF16)
+            term[c][w * n // 8 : (w + 1) * n // 8] = value.reshape(n // 8, 2, rows, LANES)
+        start_level(c, 0)
+        events(c)
+
+    dkeys = (dk_s[...] * scale).astype(BF16)
+    dvalues = dv_s[...].astype(BF16)
+    fsend[...] = (
+        (mm_nt(dkeys, wk[...]) + mm_nt(dvalues, wv[...])).astype(BF16).reshape(n, part, width)
+    )
+    ret = exchange(fsend, frecv, ret_ss, ret_rs)
+    frecv[me] = fsend[me]
+    for t in range(chunks, steps + chunks):
+        events(t)
+        if t == chunks:
             grad_latent[...] = mm_nt(dq_s[...], wq[...]).astype(BF16)
-        if t == 1:
+        if t == chunks + 1:
+            attn_s[...] = attnt_s[...].T
             attended[...] = mm(attn_s[...], wo[...]).astype(BF16)
-        if t == 2:
+        if t == chunks + 2:
             for copy in ret:
                 copy.wait()
             grad_obs[...] = mm_tn(place[...], frecv[...].reshape(key_rows, width)).astype(BF16)
@@ -385,11 +439,41 @@
         copy.wait_send()
 
 
+def move(*refs):
+    k = len(refs) // 3
+    ins, outs, bufs = refs[:k], refs[k : 2 * k], refs[2 * k : 3 * k]
+    in_sem, out_sem = refs[3 * k :]
+    loads = [pltpu.make_async_copy(ins[i], bufs[i], in_sem.at[i]) for i in range(k)]
+    stores = [pltpu.make_async_copy(bufs[i], outs[i], out_sem.at[i]) for i in range(k)]
+    for load in loads:
+        load.start()
+    for load, store in zip(loads, stores):
+        load.wait()
+        store.start()
+    for store in stores:
+        store.wait()
+
+
+def hand_out(results):
+    far = pl.BlockSpec(memory_space=pltpu.HBM)
+    k = len(results)
+    return pl.pallas_call(
+        move,
+        out_shape=tuple(jax.ShapeDtypeStruct(r.shape, r.dtype) for r in results),
+        in_specs=[far] * k,
+        out_specs=(far,) * k,
+        scratch_shapes=[pltpu.VMEM(r.shape, r.dtype) for r in results]
+        + [pltpu.SemaphoreType.DMA((k,)), pltpu.SemaphoreType.DMA((k,))],
+        compiler_params=pltpu.CompilerParams(vmem_limit_bytes=60 * 1024 * 1024),
+        name="hand_out",
+    )(*results)
+
+
 def per_device(n, g, *args):
     latent, feat, bias, route, tmask, wq, wk, wv, wo, gout = args
     lat_rows, width = latent.shape
     obs_rows = feat.shape[0]
-    blocks = route.shape[0]
+    blocks, tiles = tmask.shape
     part = CAP * (obs_rows // blocks)
     key_rows = n * part
     chunks = width // LANES
@@ -398,7 +482,19 @@
     two_step = (rows // g) % 16 == 0
     vm = pltpu.VMEM
     sem = pltpu.SemaphoreType.DMA
+    weight = vm((width, width), BF16)
     scratch = [
+        vm((lat_rows, width), BF16),
+        vm((obs_rows, width), BF16),
+        weight,
+        weight,
+        weight,
+        weight,
+        vm((lat_rows, width), BF16),
+        sem((7,)),
+        vm((width, lat_rows), BF16),
+        vm((width, key_rows), BF16),
+        vm((HEADS, key_rows, lat_rows), F32),
         vm((n, part, width + LANES), BF16),
         vm((n, part, width + LANES), BF16),
         vm((key_rows, obs_rows), BF16),
@@ -448,7 +544,8 @@
     scratch.append(vm((chunks, zr, LANES), BF16))
     scratch.append(vm((chunks, g, zr, LANES), BF16))
     spec = pl.BlockSpec(memory_space=pltpu.VMEM)
-    return pl.pallas_call(
+    far = pl.BlockSpec(memory_space=pltpu.HBM)
+    results = pl.pallas_call(
         functools.partial(kernel, n, g),
         out_shape=(
             jax.ShapeDtypeStruct((lat_rows, width), BF16),
@@ -456,14 +553,15 @@
             jax.ShapeDtypeStruct((obs_rows, width), BF16),
             jax.ShapeDtypeStruct((rows, width), F32),
         ),
-        in_specs=[spec] * 10,
+        in_specs=[far, far, spec, spec, spec, far, far, far, far, far],
         out_specs=(spec,) * 4,
         scratch_shapes=scratch,
         compiler_params=pltpu.CompilerParams(
             collective_id=0, has_side_effects=True, vmem_limit_bytes=60 * 1024 * 1024
         ),
         name="fused_layer",
-    )(latent, feat, bias.reshape(1, obs_rows), route, tmask, wq, wk, wv, wo, gout)
+    )(latent, feat, bias.reshape(1, obs_rows), route.T, tmask.T, wq, wk, wv, wo, gout)
+    return hand_out(results)
 
 
 def solution(mesh):

time: 58.6 us -> 57.6 us (0.983)
  local copies, waits for them, and re-layouts: 6.38 us -> 0 us
  Pallas kernels: 51.3 us -> 56.8 us
    unnamed x16 -> x0, local copies, waits for them, and re-layouts: 6.38 us -> none
    pallas_call x1, Pallas kernels: 51.3 us -> 54.5 us  [per_device(): pl.pallas_call(functools.partial(kernel, n, g), out_shape=(jax.ShapeDtype...]
    pallas_call x0 -> x1, Pallas kernels: none -> 2.29 us  [hand_out(): pl.pallas_call(move, out_shape=tuple((jax.ShapeDtypeStruct(r.shape, r.dty...]
where the time goes in v2:
time: 57.6 us; the launch traced here: 57.4 us
  Pallas kernels  56.8 us (99%)
  between operations  0.64 us (1%)
    pallas_call x1, Pallas kernels, per_device(): pl.pallas_call(functools.partial(kernel, n, g), out_shape=(jax.ShapeDtype...  54.5 us
    pallas_call x1, Pallas kernels, hand_out(): pl.pallas_call(move, out_shape=tuple((jax.ShapeDtypeStruct(r.shape, r.dty...  2.29 us

profile of v2, /device:TPU:0, one launch (start us, length us, event | category | flops | bytes accessed | tf_op | source)
XLA Modules:
  0.0 57.4 jit_solution(14388139916469132454)
XLA Ops:
  0.6 54.5 %fused_layer.1 = (bf16[512,512]{1,0:T(8,128)(2,1)}, bf16[512,512]{1,0:T(8,128)(2,1)}, bf16[128,512]{1,0:T(8,128)(2,1)}, f32[256,512]{1,0:T(8,128)}) custom-call(bf16[512,512]{1,0:T(8,128)(2,1)} %latent_h.1, bf16[128,512]{1,0:T(8,128)(2,1)} %feat_h.1, bf16[1,128]{1,0:T(2,128)(2,1)} %bitcast.4, s32[1,16]{1,0:T(1,128)} %bitcast.5, s32[8,16]{1,0:T(8,128)} %bitcast.3, ...), custom_call_target="tpu_custom_call" | custom-call | tf_op jit(solution)/shard_map/fused_layer/pallas_call | solution.py:548
  55.1 2.3 %hand_out.1 = (bf16[512,512]{1,0:T(8,128)(2,1)}, bf16[512,512]{1,0:T(8,128)(2,1)}, bf16[128,512]{1,0:T(8,128)(2,1)}, f32[256,512]{1,0:T(8,128)}) custom-call(bf16[512,512]{1,0:T(8,128)(2,1)} %get-tuple-element.8.refs_0_, bf16[512,512]{1,0:T(8,128)(2,1)} %get-tuple-element.9.refs_1_, bf16[128,512]{1,0:T(8,128)(2,1)} %get-tuple-element.10.refs_2_, ...), custom_call_target="tpu_custom_call" | custom-call | tf_op jit(solution)/shard_map/hand_out/pallas_call | solution.py:460

commit v3 on v2

--- a/solution.py
+++ b/solution.py
@@ -222,7 +222,7 @@
 
     gw = min(256, width)
     per_group = gw // head
-    unroll = 2
+    unroll = 4
     heads_per_chunk = LANES // head
 
     def place_of(grp_at, local):

time: 57.6 us -> 56.7 us (0.984)
  Pallas kernels: 56.8 us -> 55.9 us
    pallas_call x1, Pallas kernels: 54.5 us -> 53.6 us  [per_device(): pl.pallas_call(functools.partial(kernel, n, g), out_shape=(jax.ShapeDtype...]
where the time goes in v3:
time: 56.7 us; the launch traced here: 56.5 us
  Pallas kernels  55.9 us (99%)
  between operations  0.64 us (1%)
    pallas_call x1, Pallas kernels, per_device(): pl.pallas_call(functools.partial(kernel, n, g), out_shape=(jax.ShapeDtype...  53.6 us
    pallas_call x1, Pallas kernels, hand_out(): pl.pallas_call(move, out_shape=tuple((jax.ShapeDtypeStruct(r.shape, r.dty...  2.29 us

profile of v3, /device:TPU:0, one launch (start us, length us, event | category | flops | bytes accessed | tf_op | source)
XLA Modules:
  0.0 56.5 jit_solution(11230477903121912938)
XLA Ops:
  0.6 53.6 %fused_layer.1 = (bf16[512,512]{1,0:T(8,128)(2,1)}, bf16[512,512]{1,0:T(8,128)(2,1)}, bf16[128,512]{1,0:T(8,128)(2,1)}, f32[256,512]{1,0:T(8,128)}) custom-call(bf16[512,512]{1,0:T(8,128)(2,1)} %latent_h.1, bf16[128,512]{1,0:T(8,128)(2,1)} %feat_h.1, bf16[1,128]{1,0:T(2,128)(2,1)} %bitcast.4, s32[1,16]{1,0:T(1,128)} %bitcast.5, s32[8,16]{1,0:T(8,128)} %bitcast.3, ...), custom_call_target="tpu_custom_call" | custom-call | tf_op jit(solution)/shard_map/fused_layer/pallas_call | solution.py:548
  54.2 2.3 %hand_out.1 = (bf16[512,512]{1,0:T(8,128)(2,1)}, bf16[512,512]{1,0:T(8,128)(2,1)}, bf16[128,512]{1,0:T(8,128)(2,1)}, f32[256,512]{1,0:T(8,128)}) custom-call(bf16[512,512]{1,0:T(8,128)(2,1)} %get-tuple-element.8.refs_0_, bf16[512,512]{1,0:T(8,128)(2,1)} %get-tuple-element.9.refs_1_, bf16[128,512]{1,0:T(8,128)(2,1)} %get-tuple-element.10.refs_2_, ...), custom_call_target="tpu_custom_call" | custom-call | tf_op jit(solution)/shard_map/hand_out/pallas_call | solution.py:460
